TPU v7x, 32 devices: a whole 2x2x4 slice. The times are simulated.
32 devices in a mesh: dp: 16 (over z, y, core), mp: 2 (over x).
Axes of the slice: x: 2, y: 2, z: 4, core: 2. Of those that a mesh axis runs over, the one named last changes fastest.
Arguments:
- inputs: bfloat16 [8192, 2048], P('dp', 'mp'), may hold values from -6 to 6
- grad_moved: bfloat16 [8192, 2048], P('dp', 'mp'), may hold values from -6 to 6
- moved: int32 [16, 4], P('dp'), may hold values from 0 to 1, as said below
- segments: int32 [8192], P('dp'), may hold values from 0 to 511, as said below
- input_norm_gain: float32 [2048], replicated, may hold values from 0.5 to 1.5
- proj_in: bfloat16 [2048, 3072], P(None, 'mp'), may hold values from -0.125 to 0.125
- proj_out: bfloat16 [1024, 2048], P('mp'), may hold values from -0.1875 to 0.1875
Outputs:
- input_gradient: bfloat16 [8192, 2048], P('dp', 'mp')
- grad_proj_in: float32 [2048, 3072], P('dp', 'mp')
- grad_proj_out: float32 [1024, 2048], P('mp', 'dp')
Inputs may be any that keep to these rules, and one draw needn't show every extreme that they name: moved[g] equals moved[g XOR (8)] for every group g: blocks are swapped between partner groups slot for slot. `segments`: within each group of 512 rows the history numbers start at 0 on its first row, never fall and rise by at most one from row to row; histories never cross groups; in some group every event is a history of its own.
All inputs are finite; a program needn't handle non-finite values.
Results may differ from a plain program's by a relative error of at most 0.011.
Values may be sent and summed in bfloat16 or wider, within the bound.
A program may use at most 128 MiB of HBM per device.

v0:
```python
import jax
import jax.numpy as jnp
from jax import lax
from jax.sharding import PartitionSpec as P

DV = 128
DQK = 64
BLOCK = 128
epsilon = 1e-05
head_floor = 1.0


def swapped(block, axis, apart):
    count = lax.axis_size(axis)
    route = []
    for low in range(count):
        high = low | 1 << apart
        if high != low and high < count:
            route += [(low, high), (high, low)]
    return lax.ppermute(block, axis, route)


def forward_heads(acts, visible, heads_here):
    span = 2 * DV + 2 * DQK
    rows = acts.shape[0]
    parts = acts.reshape(rows, heads_here, span)
    u_vals = parts[:, :, :DV]
    v_vals = parts[:, :, DV : 2 * DV]
    q_vals = parts[:, :, 2 * DV : 2 * DV + DQK]
    k_vals = parts[:, :, 2 * DV + DQK :]
    scores = jnp.einsum("qhd,khd->hqk", q_vals, k_vals, preferred_element_type=jnp.float32)
    sig_s = jax.nn.sigmoid(scores)
    attend = (scores * sig_s * visible[None]).astype(jnp.bfloat16)
    slope = sig_s * (1.0 + scores * (1.0 - sig_s))
    outvals = jnp.einsum("hqk,khd->qhd", attend, v_vals, preferred_element_type=jnp.float32)
    mean_shifted = outvals - jnp.mean(outvals, axis=-1, keepdims=True)
    head_inv = lax.rsqrt(jnp.mean(mean_shifted * mean_shifted, axis=-1, keepdims=True) + head_floor)
    onorm = mean_shifted * head_inv
    mixed = (onorm * u_vals).astype(jnp.bfloat16).reshape(rows, heads_here * DV)
    saved = (u_vals, v_vals, q_vals, k_vals, attend, slope, onorm, head_inv)
    return (mixed, saved)


def backward_heads(saved, grad_mix, visible, heads_here):
    u_vals, v_vals, q_vals, k_vals, attend, slope, onorm, head_inv = saved
    rows = grad_mix.shape[0]
    grad_mixr = grad_mix.reshape(rows, heads_here, DV)
    grad_u = grad_mixr * onorm
    gon = grad_mixr * u_vals
    grad_o = (
        head_inv
        * (
            gon
            - jnp.mean(gon, axis=-1, keepdims=True)
            - onorm * jnp.mean(gon * onorm, axis=-1, keepdims=True)
        )
    ).astype(jnp.bfloat16)
    grad_att = jnp.einsum("qhd,khd->hqk", grad_o, v_vals, preferred_element_type=jnp.float32)
    grad_v = jnp.einsum("hqk,qhd->khd", attend, grad_o, preferred_element_type=jnp.float32)
    grad_scores = (grad_att * visible[None] * slope).astype(jnp.bfloat16)
    grad_q = jnp.einsum("hqk,khd->qhd", grad_scores, k_vals, preferred_element_type=jnp.float32)
    grad_k = jnp.einsum("hqk,qhd->khd", grad_scores, q_vals, preferred_element_type=jnp.float32)
    grad_act = jnp.concatenate([grad_u, grad_v, grad_q, grad_k], axis=-1)
    return grad_act.reshape(rows, heads_here * (2 * DV + 2 * DQK))


def on_device(inputs, grad_moved, moved, segments, input_norm_gain, proj_in, proj_out):
    rows = inputs.shape[0]
    span = 2 * DV + 2 * DQK
    heads_here = proj_in.shape[1] // span
    top_bit = lax.axis_size("dp").bit_length() - 2
    partner = swapped(grad_moved, "dp", top_bit)
    blocks = rows // BLOCK
    flags = moved[0][:, None, None] == 1
    returned = jnp.where(
        flags, partner.reshape(blocks, BLOCK, -1), grad_moved.reshape(blocks, BLOCK, -1)
    ).reshape(rows, -1)
    full_x, full_dy = (
        lax.all_gather(inputs, "mp", axis=1, tiled=True),
        lax.all_gather(returned, "mp", axis=1, tiled=True),
    )
    xfull = full_x.astype(jnp.float32)
    mean_shifted = xfull - jnp.mean(xfull, axis=1, keepdims=True)
    inverse_deviation = lax.rsqrt(
        jnp.mean(mean_shifted * mean_shifted, axis=1, keepdims=True) + epsilon
    )
    standardized_input = mean_shifted * inverse_deviation
    normalized_rows = (standardized_input * input_norm_gain[None, :]).astype(jnp.bfloat16)
    pre = jnp.dot(normalized_rows, proj_in, preferred_element_type=jnp.float32)
    sig_p = jax.nn.sigmoid(pre)
    acts = (pre * sig_p).astype(jnp.bfloat16)
    grad_mix = lax.dot_general(
        full_dy, proj_out, (((1,), (1,)), ((), ())), preferred_element_type=jnp.float32
    )
    order = jnp.arange(rows, dtype=jnp.int32)
    visible = (
        (segments[:, None] == segments[None, :]) & (order[None, :] <= order[:, None])
    ).astype(jnp.float32)
    mixed, saved = forward_heads(acts, visible, heads_here)
    grad_act = backward_heads(saved, grad_mix, visible, heads_here)
    partial_out = lax.dot_general(
        mixed, full_dy, (((0,), (0,)), ((), ())), preferred_element_type=jnp.float32
    )
    grad_proj_out = lax.psum_scatter(partial_out, "dp", scatter_dimension=1, tiled=True)
    grad_pre = (grad_act * sig_p * (1.0 + pre * (1.0 - sig_p))).astype(jnp.bfloat16)
    partial_in = lax.dot_general(
        normalized_rows, grad_pre, (((0,), (0,)), ((), ())), preferred_element_type=jnp.float32
    )
    grad_proj_in = lax.psum_scatter(partial_in, "dp", scatter_dimension=0, tiled=True)
    normed_term = lax.dot_general(
        grad_pre, proj_in, (((1,), (1,)), ((), ())), preferred_element_type=jnp.float32
    )
    local = inputs.shape[1]
    offset = lax.axis_index("mp") * local
    grad_normed = lax.psum(normed_term.astype(jnp.bfloat16), "mp").astype(jnp.float32)
    gain_scaled = grad_normed * input_norm_gain[None, :]
    grad_full = full_dy.astype(jnp.float32) + inverse_deviation * (
        gain_scaled
        - jnp.mean(gain_scaled, axis=1, keepdims=True)
        - standardized_input * jnp.mean(gain_scaled * standardized_input, axis=1, keepdims=True)
    )
    input_gradient = lax.dynamic_slice_in_dim(grad_full, offset, local, 1).astype(jnp.bfloat16)
    return (input_gradient, grad_proj_in, grad_proj_out)


def solution(mesh):
    return jax.shard_map(
        on_device,
        mesh=mesh,
        in_specs=(
            P("dp", "mp"),
            P("dp", "mp"),
            P("dp", None),
            P("dp"),
            P(),
            P(None, "mp"),
            P("mp", None),
        ),
        out_specs=(P("dp", "mp"), P("dp", "mp"), P("mp", "dp")),
        check_vma=False,
    )
```

profile of v0, /device:TPU:0, one launch (start us, length us, event | category | flops | bytes accessed | tf_op | source)
XLA Modules:
  0.0 408.2 jit_solution(3940126649149491493)
XLA Ops:
  7.2 0.7 all-gather.5.cloned.1.call-update
  8.0 4.1 %collective-permute-start = (bf16[512,1024]{1,0:T(8,128)(2,1)}, bf16[512,1024]{1,0:T(8,128)(2,1)S(1)}, u32[]{:S(2)}, u32[]{:S(2)}) collective-permute-start(bf16[512,1024]{1,0:T(8,128)(2,1)} %param.8), channel_id=1, source_target_pairs={{0,16},{16,0},{2,18},{18,2},{4,20},{20,4},{6,22},{22,6},{8,24},{24... | collective-permute-start | bytes 3145736 | tf_op jit(solution)/shard_map/ppermute | solution.py:20
  12.1 0.7 compare_bitcast_fusion
  12.8 0.9 fusion.10
  13.8 44.2 %collective-permute-done = bf16[512,1024]{1,0:T(8,128)(2,1)S(1)} collective-permute-done((bf16[512,1024]{1,0:T(8,128)(2,1)}, bf16[512,1024]{1,0:T(8,128)(2,1)S(1)}, u32[]{:S(2)}, u32[]{:S(2)}) %collective-permute-start) | collective-permute-done | bytes 1048608 | tf_op jit(solution)/shard_map/ppermute | solution.py:20
  57.9 2.4 broadcast_select_fusion
  60.5 2.1 convert_reduce_fusion
  62.7 0.7 fusion.2
  63.4 8.2 %multiply_convert_fusion.4 = (bf16[512,1536]{1,0:T(8,128)(2,1)}, f32[512,1536]{1,0:T(8,128)}) fusion(bf16[2048,1536]{1,0:T(8,128)(2,1)} %param.12, f32[2048]{0:T(1024)S(1)} %copy-done.13, f32[512]{0:T(512)S(1)} %add_rsqrt_fusion.1, f32[512]{0:T(512)S(1)} %broadcast_multiply_fusion.5, bf16[512,2048]{1,0:T(8,128)(2,1)S(1)} %copy-done.2), kind=kOutput, calls=%fused_computation.13 | convolution fusion | flops 3230400512 | bytes 13119488 | tf_op jit(solution)/shard_map/dot_general | solution.py:89
  71.5 2.6 copy.20
  74.1 4.3 %multiply_convert_fusion.1 = (bf16[4,512,512]{2,1,0:T(8,128)(2,1)S(1)}, f32[4,512,512]{2,1,0:T(8,128)}) fusion(f32[512,512]{1,0:T(8,128)S(1)} %fusion.10, bf16[512,4,384]{0,2,1:T(8,128)(2,1)} %bitcast.35), kind=kOutput, calls=%fused_computation.8 | convolution fusion | flops 140509184 | bytes 7864320 | tf_op jit(solution)/shard_map/qhd,khd->hqk/dot_general | solution.py:31
  78.4 1.4 copy-done.5
  79.8 1.9 fusion.24
  81.8 13.0 %all-gather.3.cloned.1.call-done = bf16[512,2048]{1,0:T(8,128)(2,1)} async-done(((bf16[512,1024]{1,0:T(8,128)(2,1)}), bf16[512,2048]{1,0:T(8,128)(2,1)}) %all-gather.3.cloned.1.call-update) | async-done | bytes 2097168 | tf_op jit(solution)/shard_map/all_gather | solution.py:80
  94.8 3.0 fusion.25
  97.8 1.2 fusion.16
  99.4 1.1 copy-done.14
  100.5 2.1 multiply_convert_fusion
  103.1 0.7 convolution_bitcast_fusion.3
  104.6 2.0 pad_maximum_fusion
  106.6 3.5 copy.19
  110.1 3.9 multiply_convert_fusion.3
  114.1 1.1 copy-done.10
  115.2 7.7 %convolution_convert_fusion = bf16[512,2048]{1,0:T(8,128)(2,1)} fusion(bf16[512,1536]{1,0:T(8,128)(2,1)S(1)} %multiply_convert_fusion.3, bf16[2048,1536]{1,0:T(8,128)(2,1)} %param.12), kind=kOutput, calls=%fused_computation.15 | convolution fusion | flops 3222274048 | bytes 9961472 | tf_op jit(solution)/shard_map/dot_general | solution.py:110
  123.2 3.2 fusion.26
  126.5 1.5 copy-done.3
  128.0 8.4 %fusion.11 = f32[2048,1536]{1,0:T(8,128)} fusion(bf16[512,1536]{1,0:T(8,128)(2,1)} %copy-done.10, f32[2048]{0:T(1024)S(1)} %copy-done.13, bf16[512,2048]{1,0:T(8,128)(2,1)S(1)} %copy-done.3, f32[512]{0:T(512)S(1)} %add_rsqrt_fusion.1, f32[512]{0:T(512)S(1)} %broadcast_multiply_fusion.5), kind=kOutput, calls=%fused_computation.38 | convolution fusion | flops 3226468352 | bytes 16265216 | tf_op jit(solution)/shard_map/dot_general | solution.py:106
  136.4 49.7 %all-reduce.2.cloned.1.call-done = bf16[512,2048]{1,0:T(8,128)(2,1)} async-done(((bf16[512,2048]{1,0:T(8,128)(2,1)}), bf16[512,2048]{1,0:T(8,128)(2,1)}) %all-reduce.2.cloned.1.call-update) | async-done | bytes 2097168 | tf_op jit(solution)/shard_map/psum | solution.py:115
  186.1 3.0 fusion.7
  189.2 1.5 fusion.6
  190.7 72.5 %reduce-scatter.5.cloned.1.call-done = f32[512,128]{1,0:T(8,128)} async-done(((f32[512,2048]{1,0:T(8,128)}), f32[512,128]{1,0:T(8,128)}) %reduce-scatter.5.cloned.1.call-update) | async-done | bytes 262160 | tf_op jit(solution)/shard_map/reduce_scatter | solution.py:104
  263.1 138.5 %reduce-scatter.3.cloned.1.call-done = f32[128,1536]{1,0:T(8,128)} async-done(((f32[2048,1536]{1,0:T(8,128)}), f32[128,1536]{1,0:T(8,128)}) %reduce-scatter.3.cloned.1.call-update) | async-done | bytes 786448 | tf_op jit(solution)/shard_map/reduce_scatter | solution.py:109
  (48 shorter events, 2.5 us)
Async XLA Ops:
  7.2 87.6 %copy-start = (bf16[512,2048]{1,0:T(8,128)(2,1)S(1)}, bf16[512,2048]{1,0:T(8,128)(2,1)}, u32[]{:S(2)}) copy-start(bf16[512,2048]{1,0:T(8,128)(2,1)} %param.13) | copy-start | bytes 6291460
  7.2 53.3 %all-gather.5.cloned.1.call-start = ((), (), s32[]{:S(2)}) async-start(), calls=%async_computation.3 | async-start | bytes 3145728 | tf_op jit(solution)/shard_map/all_gather | solution.py:79
  7.9 86.9 %all-gather.3.cloned.1.call-start = ((), (), s32[]{:S(2)}) async-start(), calls=%async_computation.2 | async-start | bytes 3145728 | tf_op jit(solution)/shard_map/all_gather | solution.py:80
  8.0 50.0 %collective-permute-start = (bf16[512,1024]{1,0:T(8,128)(2,1)}, bf16[512,1024]{1,0:T(8,128)(2,1)S(1)}, u32[]{:S(2)}, u32[]{:S(2)}) collective-permute-start(bf16[512,1024]{1,0:T(8,128)(2,1)} %param.8), channel_id=1, source_target_pairs={{0,16},{16,0},{2,18},{18,2},{4,20},{20,4},{6,22},{22,6},{8,24},{24... | collective-permute-start | bytes 3145736 | tf_op jit(solution)/shard_map/ppermute | solution.py:20
  13.8 60.4 %copy-start.11 = (f32[512,512]{1,0:T(8,128)}, f32[512,512]{1,0:T(8,128)S(1)}, u32[]{:S(2)}) copy-start(f32[512,512]{1,0:T(8,128)S(1)} %fusion.10) | copy-start | bytes 3145732
  60.3 3.0 copy-start.13
  60.4 125.7 %all-reduce.2.cloned.1.call-start = ((), (), s32[]{:S(2)}) async-start(), calls=%async_computation.4 | async-start | bytes 4194304 | tf_op jit(solution)/shard_map/psum | solution.py:115
  60.4 2.2 copy-start.2
  78.4 1.4 copy-start.5
  94.8 3.0 copy-start.4
  97.8 1.6 copy-start.12
  97.8 2.7 copy-start.14
  102.6 1.6 copy-start.6
  114.1 1.1 copy-start.10
  115.2 8.0 %copy-start.7 = (bf16[512,2048]{1,0:T(8,128)(2,1)S(1)}, bf16[512,2048]{1,0:T(8,128)(2,1)}, u32[]{:S(2)}) copy-start(bf16[512,2048]{1,0:T(8,128)(2,1)} %all-gather.3.cloned.1.call-done) | copy-start | bytes 6291460
  115.2 8.0 %copy-start.9 = (bf16[512,4,128]{0,2,1:T(8,128)(2,1)S(1)}, bf16[512,4,128]{0,2,1:T(8,128)(2,1)}, u32[]{:S(2)}) copy-start(bf16[512,4,128]{0,2,1:T(8,128)(2,1)} %get-tuple-element.7) | copy-start | bytes 1572868
  122.9 140.2 %reduce-scatter.5.cloned.1.call-start = ((), (), s32[]{:S(2)}) async-start(), calls=%async_computation.6 | async-start | bytes 4456448 | tf_op jit(solution)/shard_map/reduce_scatter | solution.py:104
  126.4 1.6 copy-start.3
  126.4 275.3 %reduce-scatter.3.cloned.1.call-start = ((), (), s32[]{:S(2)}) async-start(), calls=%async_computation.5 | async-start | bytes 13369344 | tf_op jit(solution)/shard_map/reduce_scatter | solution.py:109
  186.1 3.1 copy-start.8
  189.1 212.5 %copy-start.1 = (bf16[512,2048]{1,0:T(8,128)(2,1)S(1)}, bf16[512,2048]{1,0:T(8,128)(2,1)}, u32[]{:S(2)}) copy-start(bf16[512,2048]{1,0:T(8,128)(2,1)} %param.13) | copy-start | bytes 6291460
Sparse Core Ops, SparseCore 0:
  9.5 35.8 all-gather.4
  60.5 34.2 all-gather.2
  123.1 62.9 all-reduce.1
  190.4 72.7 reduce-scatter.4
  267.6 134.0 reduce-scatter.2
where the time goes:
time: 409 us; the launch traced here: 408 us
  waiting for transfers between devices  319 us (78%)
  matrix products  40.3 us (10%)
  other arithmetic  19 us (5%)
  between operations  14 us (3%)
  local copies, waits for them, and re-layouts  11.9 us (3%)
  starting transfers between devices  4.51 us (1%)
    reduce_scatter x1, waiting for transfers between devices, on_device(): lax.psum_scatter(partial_in, 'dp', scatter_dimension=0, tiled=True)  139 us
    reduce_scatter x1, waiting for transfers between devices, on_device(): lax.psum_scatter(partial_out, 'dp', scatter_dimension=1, tiled=True)  72.5 us
    psum x1, waiting for transfers between devices, on_device(): lax.psum(normed_term.astype(jnp.bfloat16), 'mp').astype(jnp.float32)  49.7 us
    ppermute x1, waiting for transfers between devices, swapped(): return lax.ppermute(block, axis, route)  44.2 us
    all_gather x1, waiting for transfers between devices, on_device(): lax.all_gather(returned, 'mp', axis=1, tiled=True)  13 us
    dot_general x1, matrix products, on_device(): lax.dot_general(normalized_rows, grad_pre, (((0,), (0,)), ((), ())), pref...  8.41 us
  transfers between devices with their start and end apart: 6, of which 5 were waited for; matrix products, arithmetic and copies ran while one was open for 10% of the time, Pallas kernels for 0%

commit v1 on v0

--- a/solution.py
+++ b/solution.py
@@ -112,7 +112,9 @@
     )
     local = inputs.shape[1]
     offset = lax.axis_index("mp") * local
-    grad_normed = lax.psum(normed_term.astype(jnp.bfloat16), "mp").astype(jnp.float32)
+    grad_normed = jnp.sum(lax.all_gather(normed_term.astype(jnp.bfloat16), "mp"), axis=0).astype(
+        jnp.float32
+    )
     gain_scaled = grad_normed * input_norm_gain[None, :]
     grad_full = full_dy.astype(jnp.float32) + inverse_deviation * (
         gain_scaled

time: 409 us -> 402 us (0.983)
  waiting for transfers between devices: 319 us -> 307 us
  other arithmetic: 19 us -> 24.1 us
    psum x1 -> x0, waiting for transfers between devices: 49.7 us -> none  [on_device(): lax.psum(normed_term.astype(jnp.bfloat16), 'mp').astype(jnp.float32)]
    all_gather x0 -> x1, waiting for transfers between devices: none -> 43.3 us  [on_device(): lax.all_gather(normed_term.astype(jnp.bfloat16), 'mp')]
    reduce_sum x0 -> x1, other arithmetic: none -> 5.09 us  [on_device(): jnp.sum(lax.all_gather(normed_term.astype(jnp.bfloat16), 'mp'), axis=0)]
    reduce_scatter x1, waiting for transfers between devices: 72.5 us -> 67.5 us  [on_device(): lax.psum_scatter(partial_out, 'dp', scatter_dimension=1, tiled=True)]
  transfers between devices with their start and end apart: 6 -> 6, of which waited for: 5 -> 5; matrix products, arithmetic and copies ran while one was open for 10% -> 11% of each run, Pallas kernels for 0% -> 0%
where the time goes in v1:
time: 402 us
  waiting for transfers between devices  307 us (76%)
  matrix products  40.5 us (10%)
  other arithmetic  24.1 us (6%)
  between operations  14 us (3%)
  local copies, waits for them, and re-layouts  12 us (3%)
  starting transfers between devices  4.51 us (1%)
    reduce_scatter x1, waiting for transfers between devices, on_device(): lax.psum_scatter(partial_in, 'dp', scatter_dimension=0, tiled=True)  138 us
    reduce_scatter x1, waiting for transfers between devices, on_device(): lax.psum_scatter(partial_out, 'dp', scatter_dimension=1, tiled=True)  67.5 us
    ppermute x1, waiting for transfers between devices, swapped(): return lax.ppermute(block, axis, route)  44.2 us
    all_gather x1, waiting for transfers between devices, on_device(): lax.all_gather(normed_term.astype(jnp.bfloat16), 'mp')  43.3 us
    all_gather x1, waiting for transfers between devices, on_device(): lax.all_gather(returned, 'mp', axis=1, tiled=True)  12.9 us
    dot_general x1, matrix products, on_device(): lax.dot_general(normalized_rows, grad_pre, (((0,), (0,)), ((), ())), pref...  8.55 us
    dot_general x1, matrix products, on_device(): pre = jnp.dot(normalized_rows, proj_in, preferred_element_type=jnp.float32)  8.21 us
  transfers between devices with their start and end apart: 6, of which 5 were waited for; matrix products, arithmetic and copies ran while one was open for 11% of the time, Pallas kernels for 0%

profile of v1, /device:TPU:0, one launch (start us, length us, event | category | flops | bytes accessed | tf_op | source)
XLA Modules:
  0.0 402.0 jit_solution(5214671095609699421)
XLA Ops:
  7.2 0.7 all-gather.7.cloned.1.call-update
  8.0 4.1 %collective-permute-start = (bf16[512,1024]{1,0:T(8,128)(2,1)}, bf16[512,1024]{1,0:T(8,128)(2,1)S(1)}, u32[]{:S(2)}, u32[]{:S(2)}) collective-permute-start(bf16[512,1024]{1,0:T(8,128)(2,1)} %param.8), channel_id=1, source_target_pairs={{0,16},{16,0},{2,18},{18,2},{4,20},{20,4},{6,22},{22,6},{8,24},{24... | collective-permute-start | bytes 3145736 | tf_op jit(solution)/shard_map/ppermute | solution.py:20
  12.8 0.9 fusion.10
  13.8 44.2 %collective-permute-done = bf16[512,1024]{1,0:T(8,128)(2,1)S(1)} collective-permute-done((bf16[512,1024]{1,0:T(8,128)(2,1)}, bf16[512,1024]{1,0:T(8,128)(2,1)S(1)}, u32[]{:S(2)}, u32[]{:S(2)}) %collective-permute-start) | collective-permute-done | bytes 1048608 | tf_op jit(solution)/shard_map/ppermute | solution.py:20
  57.9 2.4 broadcast_select_fusion
  60.5 2.1 convert_reduce_fusion
  62.7 0.7 fusion.2
  63.4 8.2 %multiply_convert_fusion.4 = (bf16[512,1536]{1,0:T(8,128)(2,1)}, f32[512,1536]{1,0:T(8,128)}) fusion(bf16[2048,1536]{1,0:T(8,128)(2,1)} %param.12, f32[2048]{0:T(1024)S(1)} %copy-done.13, f32[512]{0:T(512)S(1)} %add_rsqrt_fusion.1, f32[512]{0:T(512)S(1)} %broadcast_multiply_fusion.5, bf16[512,2048]{1,0:T(8,128)(2,1)S(1)} %copy-done.2), kind=kOutput, calls=%fused_computation.13 | convolution fusion | flops 3230400512 | bytes 13119488 | tf_op jit(solution)/shard_map/dot_general | solution.py:89
  71.6 2.6 copy.20
  74.2 4.3 %multiply_convert_fusion.1 = (bf16[4,512,512]{2,1,0:T(8,128)(2,1)S(1)}, f32[4,512,512]{2,1,0:T(8,128)}) fusion(f32[512,512]{1,0:T(8,128)S(1)} %fusion.10, bf16[512,4,384]{0,2,1:T(8,128)(2,1)} %bitcast.36), kind=kOutput, calls=%fused_computation.8 | convolution fusion | flops 140509184 | bytes 7864320 | tf_op jit(solution)/shard_map/qhd,khd->hqk/dot_general | solution.py:31
  78.5 1.4 copy-done.5
  79.8 1.9 fusion.24
  81.9 12.9 %all-gather.5.cloned.1.call-done = bf16[512,2048]{1,0:T(8,128)(2,1)} async-done(((bf16[512,1024]{1,0:T(8,128)(2,1)}), bf16[512,2048]{1,0:T(8,128)(2,1)}) %all-gather.5.cloned.1.call-update) | async-done | bytes 2097168 | tf_op jit(solution)/shard_map/all_gather | solution.py:80
  94.8 3.0 fusion.25
  97.8 1.2 fusion.16
  99.4 1.1 copy-done.14
  100.5 2.1 multiply_convert_fusion
  103.1 0.7 convolution_bitcast_fusion.3
  104.6 2.0 pad_maximum_fusion
  106.6 3.5 copy.19
  110.1 3.9 multiply_convert_fusion.3
  114.1 1.2 copy-done.10
  115.3 7.7 %convolution_convert_fusion = bf16[512,2048]{1,0:T(8,128)(2,1)} fusion(bf16[512,1536]{1,0:T(8,128)(2,1)S(1)} %multiply_convert_fusion.3, bf16[2048,1536]{1,0:T(8,128)(2,1)} %param.12), kind=kOutput, calls=%fused_computation.15 | convolution fusion | flops 3222274048 | bytes 9961472 | tf_op jit(solution)/shard_map/dot_general | solution.py:110
  123.3 3.2 fusion.26
  126.5 1.5 copy-done.3
  128.0 8.5 %fusion.11 = f32[2048,1536]{1,0:T(8,128)} fusion(bf16[512,1536]{1,0:T(8,128)(2,1)} %copy-done.10, f32[2048]{0:T(1024)S(1)} %copy-done.13, bf16[512,2048]{1,0:T(8,128)(2,1)S(1)} %copy-done.3, f32[512]{0:T(512)S(1)} %add_rsqrt_fusion.1, f32[512]{0:T(512)S(1)} %broadcast_multiply_fusion.5), kind=kOutput, calls=%fused_computation.38 | convolution fusion | flops 3226468352 | bytes 16265216 | tf_op jit(solution)/shard_map/dot_general | solution.py:106
  136.6 43.3 %all-gather.9.cloned.1.call-done = bf16[1024,2048]{1,0:T(8,128)(2,1)} async-done(((bf16[512,2048]{1,0:T(8,128)(2,1)}), bf16[1024,2048]{1,0:T(8,128)(2,1)}) %all-gather.9.cloned.1.call-update) | async-done | bytes 4194320 | tf_op jit(solution)/shard_map/all_gather | solution.py:115
  179.9 5.1 %reduce_sum.90 = bf16[512,2048]{1,0:T(8,128)(2,1)} reduce(bf16[2,512,2048]{2,1,0:T(8,128)(2,1)} %bitcast.43, bf16[]{:T(256)} %constant.29.clone.1), dimensions={0}, to_apply=%region_6.7 | reduce | flops 1048576 | bytes 6291458 | tf_op jit(solution)/shard_map/reduce_sum | solution.py:115
  185.0 3.0 fusion.7
  188.1 1.5 fusion.6
  189.6 67.5 %reduce-scatter.5.cloned.1.call-done = f32[512,128]{1,0:T(8,128)} async-done(((f32[512,2048]{1,0:T(8,128)}), f32[512,128]{1,0:T(8,128)}) %reduce-scatter.5.cloned.1.call-update) | async-done | bytes 262160 | tf_op jit(solution)/shard_map/reduce_scatter | solution.py:104
  257.0 138.4 %reduce-scatter.3.cloned.1.call-done = f32[128,1536]{1,0:T(8,128)} async-done(((f32[2048,1536]{1,0:T(8,128)}), f32[128,1536]{1,0:T(8,128)}) %reduce-scatter.3.cloned.1.call-update) | async-done | bytes 786448 | tf_op jit(solution)/shard_map/reduce_scatter | solution.py:109
  (49 shorter events, 3.2 us)
Async XLA Ops:
  7.2 87.6 %copy-start = (bf16[512,2048]{1,0:T(8,128)(2,1)S(1)}, bf16[512,2048]{1,0:T(8,128)(2,1)}, u32[]{:S(2)}) copy-start(bf16[512,2048]{1,0:T(8,128)(2,1)} %param.13) | copy-start | bytes 6291460
  7.2 53.3 %all-gather.7.cloned.1.call-start = ((), (), s32[]{:S(2)}) async-start(), calls=%async_computation.3 | async-start | bytes 3145728 | tf_op jit(solution)/shard_map/all_gather | solution.py:79
  7.9 86.9 %all-gather.5.cloned.1.call-start = ((), (), s32[]{:S(2)}) async-start(), calls=%async_computation.2 | async-start | bytes 3145728 | tf_op jit(solution)/shard_map/all_gather | solution.py:80
  8.0 50.0 %collective-permute-start = (bf16[512,1024]{1,0:T(8,128)(2,1)}, bf16[512,1024]{1,0:T(8,128)(2,1)S(1)}, u32[]{:S(2)}, u32[]{:S(2)}) collective-permute-start(bf16[512,1024]{1,0:T(8,128)(2,1)} %param.8), channel_id=1, source_target_pairs={{0,16},{16,0},{2,18},{18,2},{4,20},{20,4},{6,22},{22,6},{8,24},{24... | collective-permute-start | bytes 3145736 | tf_op jit(solution)/shard_map/ppermute | solution.py:20
  13.8 60.4 %copy-start.11 = (f32[512,512]{1,0:T(8,128)}, f32[512,512]{1,0:T(8,128)S(1)}, u32[]{:S(2)}) copy-start(f32[512,512]{1,0:T(8,128)S(1)} %fusion.10) | copy-start | bytes 3145732
  60.3 3.0 copy-start.13
  60.4 119.5 %all-gather.9.cloned.1.call-start = ((), (), s32[]{:S(2)}) async-start(), calls=%async_computation.6 | async-start | bytes 6291456 | tf_op jit(solution)/shard_map/all_gather | solution.py:115
  60.4 2.2 copy-start.2
  78.5 1.4 copy-start.5
  94.8 3.0 copy-start.4
  97.8 1.6 copy-start.12
  97.8 2.7 copy-start.14
  102.6 1.6 copy-start.6
  114.1 1.2 copy-start.10
  115.3 7.9 %copy-start.7 = (bf16[512,2048]{1,0:T(8,128)(2,1)S(1)}, bf16[512,2048]{1,0:T(8,128)(2,1)}, u32[]{:S(2)}) copy-start(bf16[512,2048]{1,0:T(8,128)(2,1)} %all-gather.5.cloned.1.call-done) | copy-start | bytes 6291460
  115.3 8.0 %copy-start.9 = (bf16[512,4,128]{0,2,1:T(8,128)(2,1)S(1)}, bf16[512,4,128]{0,2,1:T(8,128)(2,1)}, u32[]{:S(2)}) copy-start(bf16[512,4,128]{0,2,1:T(8,128)(2,1)} %get-tuple-element.7) | copy-start | bytes 1572868
  123.0 134.0 %reduce-scatter.5.cloned.1.call-start = ((), (), s32[]{:S(2)}) async-start(), calls=%async_computation.5 | async-start | bytes 4456448 | tf_op jit(solution)/shard_map/reduce_scatter | solution.py:104
  126.5 1.6 copy-start.3
  126.5 269.0 %reduce-scatter.3.cloned.1.call-start = ((), (), s32[]{:S(2)}) async-start(), calls=%async_computation.4 | async-start | bytes 13369344 | tf_op jit(solution)/shard_map/reduce_scatter | solution.py:109
  185.0 3.1 copy-start.8
  188.0 207.4 %copy-start.1 = (bf16[512,2048]{1,0:T(8,128)(2,1)S(1)}, bf16[512,2048]{1,0:T(8,128)(2,1)}, u32[]{:S(2)}) copy-start(bf16[512,2048]{1,0:T(8,128)(2,1)} %param.13) | copy-start | bytes 6291460
Sparse Core Ops, SparseCore 0:
  9.5 35.8 all-gather.6
  60.5 34.2 all-gather.4
  123.1 56.7 all-gather.8
  184.2 72.8 reduce-scatter.4
  261.5 133.9 reduce-scatter.2
